TPU v7x, 32 devices: a whole 2x2x4 slice. The times are simulated.
32 devices in a mesh: seq: 8 (over z, core), grp: 4 (over y, x).
Axes of the slice: x: 2, y: 2, z: 4, core: 2. Of those that a mesh axis runs over, the one named last changes fastest.
Arguments:
- tokens: bfloat16 [65536, 1280], P(('seq', 'grp')), may hold values from -27 to 27
- slot_keys: bfloat16 [1280, 128], replicated, may hold values from -1.5 to 1.5
- norm_gain: float32 [32, 1280], P(('seq', 'grp')), may hold values from 0.1 to 1.9
- w_in: bfloat16 [32, 1280, 2560], P(('seq', 'grp')), may hold values from -0.15625 to 0.15625
- w_out: bfloat16 [32, 2560, 1280], P(('seq', 'grp')), may hold values from -0.125 to 0.125
Outputs:
- mixed: bfloat16 [65536, 1280], P(('seq', 'grp'))
All inputs are finite; a program needn't handle non-finite values.
Results may differ from a plain program's by a relative error of at most 0.007.
Values may be sent and summed in bfloat16 or wider, within the bound.
No kernel may reach another device: no remote copies, remote signals or barrier semaphores. Data moves between devices by JAX's collectives and lax.ppermute only.
A program may use at most 128 MiB of HBM per device.

v0:
```python
import jax
import jax.numpy as jnp
from jax import lax
from jax.sharding import PartitionSpec as P


def on_device(tokens, slot_keys, norm_gain, w_in, w_out):
    devices = lax.axis_size(("seq", "grp"))
    logits = jnp.dot(tokens, slot_keys, preferred_element_type=jnp.float32)
    per_dev = logits.shape[1] // devices
    maxima = jnp.max(logits, axis=0)
    scores = jnp.exp(logits - maxima[None, :])
    totals = jnp.sum(scores, axis=0)
    weights = scores.astype(jnp.bfloat16)
    dims = (((0,), (0,)), ((), ()))
    numer_local = lax.dot_general(weights, tokens, dims, preferred_element_type=jnp.float32)
    parts, peaks, sums = (
        lax.all_to_all(numer_local, ("seq", "grp"), split_axis=0, concat_axis=0, tiled=True),
        lax.all_to_all(maxima, ("seq", "grp"), split_axis=0, concat_axis=0, tiled=True),
        lax.all_to_all(totals, ("seq", "grp"), split_axis=0, concat_axis=0, tiled=True),
    )
    peaks = peaks.reshape(devices, per_dev)
    factor = jnp.exp(peaks - jnp.max(peaks, axis=0, keepdims=True))
    numer = jnp.sum(parts.reshape(devices, per_dev, -1) * factor[:, :, None], axis=0)
    own_total = jnp.sum(sums.reshape(devices, per_dev) * factor, axis=0)
    slot_in = numer / own_total[:, None]
    normed = (slot_in * norm_gain[0][None, :]).astype(jnp.bfloat16)
    hidden = jax.nn.gelu(jnp.dot(normed, w_in[0], preferred_element_type=jnp.float32)).astype(
        jnp.bfloat16
    )
    expert_out = jnp.dot(hidden, w_out[0], preferred_element_type=jnp.float32).astype(jnp.bfloat16)
    row_top = jnp.max(logits, axis=1, keepdims=True)
    row_exp = jnp.exp(logits - row_top)
    combine = (row_exp / jnp.sum(row_exp, axis=1, keepdims=True)).astype(jnp.bfloat16)
    gathered = lax.all_gather(expert_out, ("seq", "grp"), axis=0, tiled=True)
    mixed = jnp.dot(combine, gathered, preferred_element_type=jnp.float32)
    return mixed.astype(jnp.bfloat16)


def solution(mesh):
    return jax.shard_map(
        on_device,
        mesh=mesh,
        in_specs=(
            P(("seq", "grp"), None),
            P(),
            P(("seq", "grp"), None),
            P(("seq", "grp"), None, None),
            P(("seq", "grp"), None, None),
        ),
        out_specs=P(("seq", "grp"), None),
        check_vma=False,
    )
```

profile of v0, /device:TPU:0, one launch (start us, length us, event | category | flops | bytes accessed | tf_op | source)
XLA Modules:
  0.0 129.9 jit_solution(6131586817786573005)
XLA Ops:
  0.0 1.0 copy-done
  1.0 4.1 %fusion.47 = (f32[2048]{0:T(1024)S(1)}, f32[128]{0:T(128)S(1)}, f32[2048,128]{1,0:T(8,128)S(1)}) fusion(bf16[2048,1280]{1,0:T(8,128)(2,1)} %param.5, bf16[1280,128]{1,0:T(8,128)(2,1)S(1)} %copy-done), kind=kOutput, calls=%fused_computation.43 | convolution fusion | flops 671610752 | bytes 6627840 | tf_op jit(solution)/shard_map/dot_general | solution.py:9
  5.1 0.6 fusion.10
  5.7 0.7 all_to_all.22
  6.4 7.3 %all-to-all-start.2 = ((f32[32,4,1]{1,2,0:T(1,128)}), f32[32,4,1]{1,2,0:T(1,128)S(1)}, u32[]{:S(2)}, u32[]{:S(2)}) async-start(f32[32,4,1]{1,2,0:T(1,128)} %bitcast.2), calls=%async_computation.2 | async-start | bytes 32768 | tf_op jit(solution)/shard_map/all_to_all | solution.py:20
  13.8 0.7 all_to_all.20
  14.5 6.4 %all-to-all-done.2 = f32[32,4,1]{1,2,0:T(1,128)S(1)} async-done(((f32[32,4,1]{1,2,0:T(1,128)}), f32[32,4,1]{1,2,0:T(1,128)S(1)}, u32[]{:S(2)}, u32[]{:S(2)}) %all-to-all-start.2) | async-done | bytes 544 | tf_op jit(solution)/shard_map/all_to_all | solution.py:20
  20.9 2.6 %all-to-all-start.1 = ((f32[32,4,1]{1,2,0:T(1,128)}), f32[32,4,1]{1,2,0:T(1,128)S(1)}, u32[]{:S(2)}, u32[]{:S(2)}) async-start(f32[32,4,1]{1,2,0:T(1,128)} %bitcast), calls=%async_computation.1 | async-start | bytes 32768 | tf_op jit(solution)/shard_map/all_to_all | solution.py:19
  23.4 3.4 %fusion.13 = f32[128,1280]{1,0:T(8,128)S(1)} fusion(bf16[2048,1280]{1,0:T(8,128)(2,1)} %param.5, f32[2048,128]{1,0:T(8,128)S(1)} %get-tuple-element.9, f32[128]{0:T(128)S(1)} %get-tuple-element.8), kind=kOutput, calls=%fused_computation.14 | convolution fusion | flops 671612928 | bytes 6947328 | tf_op jit(solution)/shard_map/dot_general | solution.py:16
  26.9 1.0 all_to_all.18
  27.9 2.8 %all-to-all-done.1 = f32[32,4,1]{1,2,0:T(1,128)S(1)} async-done(((f32[32,4,1]{1,2,0:T(1,128)}), f32[32,4,1]{1,2,0:T(1,128)S(1)}, u32[]{:S(2)}, u32[]{:S(2)}) %all-to-all-start.1) | async-done | bytes 544 | tf_op jit(solution)/shard_map/all_to_all | solution.py:19
  30.6 3.1 %all-to-all-start = ((f32[32,4,1280]{2,1,0:T(4,128)}), f32[32,4,1280]{2,1,0:T(4,128)S(1)}, u32[]{:S(2)}, u32[]{:S(2)}) async-start(f32[32,4,1280]{2,1,0:T(4,128)} %all_to_all.18), calls=%async_computation | async-start | bytes 1310720 | tf_op jit(solution)/shard_map/all_to_all | solution.py:18
  33.8 0.1 copy.21
  33.8 0.1 reduce_max.29
  33.9 0.1 exponential_bitcast_fusion
  34.0 0.1 copy.22
  34.1 0.1 copy.24
  34.1 0.2 fusion.42
  34.3 18.3 %all-to-all-done = f32[32,4,1280]{2,1,0:T(4,128)S(1)} async-done(((f32[32,4,1280]{2,1,0:T(4,128)}), f32[32,4,1280]{2,1,0:T(4,128)S(1)}, u32[]{:S(2)}, u32[]{:S(2)}) %all-to-all-start) | async-done | bytes 655392 | tf_op jit(solution)/shard_map/all_to_all | solution.py:18
  52.6 0.2 multiply_reduce_fusion
  52.8 6.7 %fusion.7 = bf16[1,4,1280]{2,1,0:T(4,128)(2,1)S(1)} fusion(bf16[1,2560,1280]{2,1,0:T(8,128)(2,1)} %param.9, bf16[1,1280,2560]{2,1,0:T(8,128)(2,1)} %param.8, f32[4,1280]{1,0:T(4,128)S(1)} %multiply_reduce_fusion, f32[1280]{0:T(1024)S(1)} %reduce.1, f32[4]{0:T(128)S(1)} %fusion.42), kind=kOutput, calls=%fused_computation.6 | convolution fusion | flops 52541440 | bytes 13143056 | tf_op jit(solution)/shard_map/dot_general | solution.py:31
  59.5 66.8 %all-gather = bf16[32,4,1280]{2,1,0:T(4,128)(2,1)S(1)} all-gather(bf16[1,4,1280]{2,1,0:T(4,128)(2,1)S(1)} %fusion.7), channel_id=1, replica_groups=mesh['seq'=8,'grp'=4] {'seq','grp'}, dimensions={0}, use_global_device_ids=true | all-gather | bytes 337920 | tf_op jit(solution)/shard_map/all_gather | solution.py:35
  126.3 0.1 reshape.31
  126.3 3.6 %convolution_convert_fusion = bf16[2048,1280]{1,0:T(8,128)(2,1)} fusion(bf16[128,1280]{1,0:T(8,128)(2,1)S(1)} %reshape.31, f32[2048,128]{1,0:T(8,128)S(1)} %get-tuple-element.9, f32[2048]{0:T(1024)S(1)} %get-tuple-element.5, f32[2048]{0:T(1024)S(1)} %get-tuple-element.7), kind=kOutput, calls=%fused_computation | convolution fusion | flops 674496512 | bytes 6635520 | tf_op jit(solution)/shard_map/dot_general | solution.py:36
  (4 shorter events, 0.0 us)
Async XLA Ops:
  0.0 1.0 copy-start
  5.1 28.7 %copy-start.1 = (f32[1,1280]{1,0:T(1,128)S(1)}, f32[1,1280]{1,0:T(1,128)}, u32[]{:S(2)}) copy-start(f32[1,1280]{1,0:T(1,128)} %param.7) | copy-start | bytes 15364
  6.4 14.5 %all-to-all-start.2 = ((f32[32,4,1]{1,2,0:T(1,128)}), f32[32,4,1]{1,2,0:T(1,128)S(1)}, u32[]{:S(2)}, u32[]{:S(2)}) async-start(f32[32,4,1]{1,2,0:T(1,128)} %bitcast.2), calls=%async_computation.2 | async-start | bytes 32768 | tf_op jit(solution)/shard_map/all_to_all | solution.py:20
  20.9 9.8 %all-to-all-start.1 = ((f32[32,4,1]{1,2,0:T(1,128)}), f32[32,4,1]{1,2,0:T(1,128)S(1)}, u32[]{:S(2)}, u32[]{:S(2)}) async-start(f32[32,4,1]{1,2,0:T(1,128)} %bitcast), calls=%async_computation.1 | async-start | bytes 32768 | tf_op jit(solution)/shard_map/all_to_all | solution.py:19
  30.6 21.9 %all-to-all-start = ((f32[32,4,1280]{2,1,0:T(4,128)}), f32[32,4,1280]{2,1,0:T(4,128)S(1)}, u32[]{:S(2)}, u32[]{:S(2)}) async-start(f32[32,4,1280]{2,1,0:T(4,128)} %all_to_all.18), calls=%async_computation | async-start | bytes 1310720 | tf_op jit(solution)/shard_map/all_to_all | solution.py:18
where the time goes:
time: 130 us
  blocking collectives  66.8 us (51%)
  waiting for transfers between devices  27.4 us (21%)
  matrix products  17.8 us (14%)
  starting transfers between devices  13 us (10%)
  local copies, waits for them, and re-layouts  3.74 us (3%)
    all_gather x1, blocking collectives, on_device(): gathered = lax.all_gather(expert_out, ('seq', 'grp'), axis=0, tiled=True)  66.8 us
    all_to_all x1, waiting for transfers between devices, on_device(): lax.all_to_all(numer_local, ('seq', 'grp'), split_axis=0, concat_axis=0,...  18.3 us
    all_to_all x1, starting transfers between devices, on_device(): lax.all_to_all(totals, ('seq', 'grp'), split_axis=0, concat_axis=0, tiled...  7.32 us
    dot_general x1, matrix products, on_device(): jnp.dot(hidden, w_out[0], preferred_element_type=jnp.float32)  6.7 us
    all_to_all x1, waiting for transfers between devices, on_device(): lax.all_to_all(totals, ('seq', 'grp'), split_axis=0, concat_axis=0, tiled...  6.42 us
    dot_general x1, matrix products, on_device(): logits = jnp.dot(tokens, slot_keys, preferred_element_type=jnp.float32)  4.08 us
    dot_general x1, matrix products, on_device(): mixed = jnp.dot(combine, gathered, preferred_element_type=jnp.float32)  3.58 us
    dot_general x1, matrix products, on_device(): lax.dot_general(weights, tokens, dims, preferred_element_type=jnp.float32)  3.4 us
  transfers between devices with their start and end apart: 3, of which 3 were waited for; matrix products, arithmetic and copies ran while one was open for 3% of the time, Pallas kernels for 0%

commit v1 on v0

--- a/solution.py
+++ b/solution.py
@@ -2,6 +2,18 @@
 import jax.numpy as jnp
 from jax import lax
 from jax.sharding import PartitionSpec as P
+
+
+def doubled_up(x, axis, dim):
+    ways, here = (lax.axis_size(axis), lax.axis_index(axis))
+    grown, reach = (x, 1)
+    while reach < ways:
+        theirs = lax.ppermute(grown, axis, [(d, d ^ reach) for d in range(ways)])
+        mine_first = jnp.concatenate([grown, theirs], axis=dim)
+        theirs_first = jnp.concatenate([theirs, grown], axis=dim)
+        grown = jnp.where(here & reach == 0, mine_first, theirs_first)
+        reach = 2 * reach
+    return grown
 
 
 def on_device(tokens, slot_keys, norm_gain, w_in, w_out):
@@ -32,7 +44,7 @@
     row_top = jnp.max(logits, axis=1, keepdims=True)
     row_exp = jnp.exp(logits - row_top)
     combine = (row_exp / jnp.sum(row_exp, axis=1, keepdims=True)).astype(jnp.bfloat16)
-    gathered = lax.all_gather(expert_out, ("seq", "grp"), axis=0, tiled=True)
+    gathered = doubled_up(expert_out, ("seq", "grp"), 0)
     mixed = jnp.dot(combine, gathered, preferred_element_type=jnp.float32)
     return mixed.astype(jnp.bfloat16)
 

time: 130 us -> 86.8 us (0.67)
  blocking collectives: 66.8 us -> 0 us
  waiting for transfers between devices: 27.4 us -> 48.3 us
  starting transfers between devices: 13 us -> 15.4 us
    all_gather x1 -> x0, blocking collectives: 66.8 us -> none  [on_device(): gathered = lax.all_gather(expert_out, ('seq', 'grp'), axis=0, tiled=True)]
    ppermute x0 -> x5, waiting for transfers between devices: none -> 20.9 us  [doubled_up(): theirs = lax.ppermute(grown, axis, [(d, d ^ reach) for d in range(ways)])]
    ppermute x0 -> x5, starting transfers between devices: none -> 2.41 us  [doubled_up(): theirs = lax.ppermute(grown, axis, [(d, d ^ reach) for d in range(ways)])]
  transfers between devices with their start and end apart: 3 -> 8, of which waited for: 3 -> 8; matrix products, arithmetic and copies ran while one was open for 3% -> 5% of each run, Pallas kernels for 0% -> 0%
where the time goes in v1:
time: 86.8 us; the launch traced here: 86.4 us
  waiting for transfers between devices  48.3 us (56%)
  matrix products  17.7 us (20%)
  starting transfers between devices  15.4 us (18%)
  local copies, waits for them, and re-layouts  3.66 us (4%)
  other arithmetic  1.25 us (1%)
    ppermute x5, waiting for transfers between devices, doubled_up(): theirs = lax.ppermute(grown, axis, [(d, d ^ reach) for d in range(ways)])  20.9 us
    all_to_all x1, waiting for transfers between devices, on_device(): lax.all_to_all(numer_local, ('seq', 'grp'), split_axis=0, concat_axis=0,...  18.3 us
    all_to_all x1, starting transfers between devices, on_device(): lax.all_to_all(totals, ('seq', 'grp'), split_axis=0, concat_axis=0, tiled...  7.32 us
    dot_general x1, matrix products, on_device(): jnp.dot(hidden, w_out[0], preferred_element_type=jnp.float32)  6.7 us
    all_to_all x1, waiting for transfers between devices, on_device(): lax.all_to_all(totals, ('seq', 'grp'), split_axis=0, concat_axis=0, tiled...  6.42 us
    dot_general x1, matrix products, on_device(): logits = jnp.dot(tokens, slot_keys, preferred_element_type=jnp.float32)  4.08 us
    dot_general x1, matrix products, on_device(): mixed = jnp.dot(combine, gathered, preferred_element_type=jnp.float32)  3.56 us
    dot_general x1, matrix products, on_device(): lax.dot_general(weights, tokens, dims, preferred_element_type=jnp.float32)  3.4 us
  transfers between devices with their start and end apart: 8, of which 8 were waited for; matrix products, arithmetic and copies ran while one was open for 5% of the time, Pallas kernels for 0%

profile of v1, /device:TPU:0, one launch (start us, length us, event | category | flops | bytes accessed | tf_op | source)
XLA Modules:
  0.0 86.4 jit_solution(7779200261501206317)
XLA Ops:
  0.0 1.0 %copy-done = bf16[1280,128]{1,0:T(8,128)(2,1)S(1)} copy-done((bf16[1280,128]{1,0:T(8,128)(2,1)S(1)}, bf16[1280,128]{1,0:T(8,128)(2,1)}, u32[]{:S(2)}) %copy-start) | copy-done | bytes 327704
  1.0 4.1 %fusion.51 = (f32[128]{0:T(128)S(1)}, f32[2048]{0:T(1024)S(1)}, f32[2048,128]{1,0:T(8,128)S(1)}) fusion(bf16[2048,1280]{1,0:T(8,128)(2,1)} %param.5, bf16[1280,128]{1,0:T(8,128)(2,1)S(1)} %copy-done), kind=kOutput, calls=%fused_computation.54 | convolution fusion | flops 671610752 | bytes 6627840 | tf_op jit(solution)/shard_map/dot_general | solution.py:21
  5.1 0.6 fusion.8
  5.7 0.7 all_to_all.22
  6.4 7.3 %all-to-all-start.2 = ((f32[32,4,1]{1,2,0:T(1,128)}), f32[32,4,1]{1,2,0:T(1,128)S(1)}, u32[]{:S(2)}, u32[]{:S(2)}) async-start(f32[32,4,1]{1,2,0:T(1,128)} %bitcast.2), calls=%async_computation.2 | async-start | bytes 32768 | tf_op jit(solution)/shard_map/all_to_all | solution.py:32
  13.8 0.7 all_to_all.20
  14.5 6.4 %all-to-all-done.2 = f32[32,4,1]{1,2,0:T(1,128)S(1)} async-done(((f32[32,4,1]{1,2,0:T(1,128)}), f32[32,4,1]{1,2,0:T(1,128)S(1)}, u32[]{:S(2)}, u32[]{:S(2)}) %all-to-all-start.2) | async-done | bytes 544 | tf_op jit(solution)/shard_map/all_to_all | solution.py:32
  20.9 2.6 %all-to-all-start.1 = ((f32[32,4,1]{1,2,0:T(1,128)}), f32[32,4,1]{1,2,0:T(1,128)S(1)}, u32[]{:S(2)}, u32[]{:S(2)}) async-start(f32[32,4,1]{1,2,0:T(1,128)} %bitcast), calls=%async_computation.1 | async-start | bytes 32768 | tf_op jit(solution)/shard_map/all_to_all | solution.py:31
  23.4 3.4 %fusion.10 = f32[128,1280]{1,0:T(8,128)S(1)} fusion(bf16[2048,1280]{1,0:T(8,128)(2,1)} %param.5, f32[2048,128]{1,0:T(8,128)S(1)} %get-tuple-element.9, f32[128]{0:T(128)S(1)} %get-tuple-element.7), kind=kOutput, calls=%fused_computation.13 | convolution fusion | flops 671612928 | bytes 6947328 | tf_op jit(solution)/shard_map/dot_general | solution.py:28
  26.9 1.0 %all_to_all.18 = f32[32,4,1280]{2,1,0:T(4,128)} reshape(f32[128,1280]{1,0:T(8,128)S(1)} %fusion.10) | data formatting | bytes 1310720 | tf_op jit(solution)/shard_map/all_to_all | solution.py:30
  27.9 2.8 %all-to-all-done.1 = f32[32,4,1]{1,2,0:T(1,128)S(1)} async-done(((f32[32,4,1]{1,2,0:T(1,128)}), f32[32,4,1]{1,2,0:T(1,128)S(1)}, u32[]{:S(2)}, u32[]{:S(2)}) %all-to-all-start.1) | async-done | bytes 544 | tf_op jit(solution)/shard_map/all_to_all | solution.py:31
  30.6 3.1 %all-to-all-start = ((f32[32,4,1280]{2,1,0:T(4,128)}), f32[32,4,1280]{2,1,0:T(4,128)S(1)}, u32[]{:S(2)}, u32[]{:S(2)}) async-start(f32[32,4,1280]{2,1,0:T(4,128)} %all_to_all.18), calls=%async_computation | async-start | bytes 1310720 | tf_op jit(solution)/shard_map/all_to_all | solution.py:30
  34.3 18.3 %all-to-all-done = f32[32,4,1280]{2,1,0:T(4,128)S(1)} async-done(((f32[32,4,1280]{2,1,0:T(4,128)}), f32[32,4,1280]{2,1,0:T(4,128)S(1)}, u32[]{:S(2)}, u32[]{:S(2)}) %all-to-all-start) | async-done | bytes 655392 | tf_op jit(solution)/shard_map/all_to_all | solution.py:30
  52.8 6.7 %fusion.4 = bf16[4,1280]{1,0:T(4,128)(2,1)S(1)} fusion(bf16[1,2560,1280]{2,1,0:T(8,128)(2,1)} %param.9, bf16[1,1280,2560]{2,1,0:T(8,128)(2,1)} %param.8, f32[4,1280]{1,0:T(4,128)S(1)} %multiply_reduce_fusion, f32[1280]{0:T(1024)S(1)} %reduce.1, f32[4]{0:T(128)S(1)} %fusion.45), kind=kOutput, calls=%fused_computation.5 | convolution fusion | flops 52541440 | bytes 13143056 | tf_op jit(solution)/shard_map/dot_general | solution.py:43
  59.5 0.4 collective-permute-start
  59.9 3.3 %collective-permute-done = bf16[4,1280]{1,0:T(4,128)(2,1)S(1)} collective-permute-done((bf16[4,1280]{1,0:T(4,128)(2,1)S(1)}, bf16[4,1280]{1,0:T(4,128)(2,1)S(1)}, u32[]{:S(2)}, u32[]{:S(2)}) %collective-permute-start) | collective-permute-done | bytes 10272 | tf_op jit(solution)/shard_map/ppermute | solution.py:11
  63.2 0.5 collective-permute-start.1
  63.7 3.4 %collective-permute-done.1 = bf16[8,1280]{1,0:T(8,128)(2,1)S(1)} collective-permute-done((bf16[8,1280]{1,0:T(8,128)(2,1)S(1)}, bf16[8,1280]{1,0:T(8,128)(2,1)S(1)}, u32[]{:S(2)}, u32[]{:S(2)}) %collective-permute-start.1) | collective-permute-done | bytes 20512 | tf_op jit(solution)/shard_map/ppermute | solution.py:11
  67.2 1.2 %collective-permute-done.2 = bf16[16,1280]{1,0:T(8,128)(2,1)S(1)} collective-permute-done((bf16[16,1280]{1,0:T(8,128)(2,1)S(1)}, bf16[16,1280]{1,0:T(8,128)(2,1)S(1)}, u32[]{:S(2)}, u32[]{:S(2)}) %collective-permute-start.2) | collective-permute-done | bytes 40992 | tf_op jit(solution)/shard_map/ppermute | solution.py:11
  68.4 1.2 %collective-permute-start.3 = (bf16[32,1280]{1,0:T(8,128)(2,1)S(1)}, bf16[32,1280]{1,0:T(8,128)(2,1)S(1)}, u32[]{:S(2)}, u32[]{:S(2)}) collective-permute-start(bf16[32,1280]{1,0:T(8,128)(2,1)S(1)} %maximum_select_fusion.3), channel_id=1, source_target_pairs={{0,8},{1,9},{2,10},{3,11},{4,12},{5,13},{6,14},{7,15},{8,0},{9,1},... | collective-permute-start | bytes 245768 | tf_op jit(solution)/shard_map/ppermute | solution.py:11
  69.5 3.4 %collective-permute-done.3 = bf16[32,1280]{1,0:T(8,128)(2,1)S(1)} collective-permute-done((bf16[32,1280]{1,0:T(8,128)(2,1)S(1)}, bf16[32,1280]{1,0:T(8,128)(2,1)S(1)}, u32[]{:S(2)}, u32[]{:S(2)}) %collective-permute-start.3) | collective-permute-done | bytes 81952 | tf_op jit(solution)/shard_map/ppermute | solution.py:11
  73.0 0.3 collective-permute-start.4
  73.3 9.6 %collective-permute-done.4 = bf16[64,1280]{1,0:T(8,128)(2,1)S(1)} collective-permute-done((bf16[64,1280]{1,0:T(8,128)(2,1)S(1)}, bf16[64,1280]{1,0:T(8,128)(2,1)S(1)}, u32[]{:S(2)}, u32[]{:S(2)}) %collective-permute-start.4) | collective-permute-done | bytes 163872 | tf_op jit(solution)/shard_map/ppermute | solution.py:11
  82.9 3.6 %convolution_convert_fusion = bf16[2048,1280]{1,0:T(8,128)(2,1)} fusion(f32[2048,128]{1,0:T(8,128)S(1)} %get-tuple-element.9, f32[2048]{0:T(1024)S(1)} %get-tuple-element.6, f32[2048]{0:T(1024)S(1)} %get-tuple-element.8, bf16[64,1280]{1,0:T(8,128)(2,1)S(1)} %collective-permute-done.4, bf16[64,1280]{1,0:T(8,128)(2,1)S(1)} %maximum_select_fusion.2, pred[]{:T(512)S(6)} %eq.15), kind=kOutput, calls=%fused_computation | convolution fusion | flops 675971072 | bytes 6635521 | tf_op jit(solution)/shard_map/dot_general | solution.py:48
  (16 shorter events, 0.9 us)
Async XLA Ops:
  0.0 1.0 %copy-start = (bf16[1280,128]{1,0:T(8,128)(2,1)S(1)}, bf16[1280,128]{1,0:T(8,128)(2,1)}, u32[]{:S(2)}) copy-start(bf16[1280,128]{1,0:T(8,128)(2,1)} %param.6) | copy-start | bytes 983044
  5.1 28.7 %copy-start.1 = (f32[1,1280]{1,0:T(1,128)S(1)}, f32[1,1280]{1,0:T(1,128)}, u32[]{:S(2)}) copy-start(f32[1,1280]{1,0:T(1,128)} %param.7) | copy-start | bytes 15364
  6.4 14.5 %all-to-all-start.2 = ((f32[32,4,1]{1,2,0:T(1,128)}), f32[32,4,1]{1,2,0:T(1,128)S(1)}, u32[]{:S(2)}, u32[]{:S(2)}) async-start(f32[32,4,1]{1,2,0:T(1,128)} %bitcast.2), calls=%async_computation.2 | async-start | bytes 32768 | tf_op jit(solution)/shard_map/all_to_all | solution.py:32
  20.9 9.8 %all-to-all-start.1 = ((f32[32,4,1]{1,2,0:T(1,128)}), f32[32,4,1]{1,2,0:T(1,128)S(1)}, u32[]{:S(2)}, u32[]{:S(2)}) async-start(f32[32,4,1]{1,2,0:T(1,128)} %bitcast), calls=%async_computation.1 | async-start | bytes 32768 | tf_op jit(solution)/shard_map/all_to_all | solution.py:31
  30.6 21.9 %all-to-all-start = ((f32[32,4,1280]{2,1,0:T(4,128)}), f32[32,4,1280]{2,1,0:T(4,128)S(1)}, u32[]{:S(2)}, u32[]{:S(2)}) async-start(f32[32,4,1280]{2,1,0:T(4,128)} %all_to_all.18), calls=%async_computation | async-start | bytes 1310720 | tf_op jit(solution)/shard_map/all_to_all | solution.py:30
  59.5 3.7 %collective-permute-start = (bf16[4,1280]{1,0:T(4,128)(2,1)S(1)}, bf16[4,1280]{1,0:T(4,128)(2,1)S(1)}, u32[]{:S(2)}, u32[]{:S(2)}) collective-permute-start(bf16[4,1280]{1,0:T(4,128)(2,1)S(1)} %fusion.4), channel_id=1, source_target_pairs={{0,1},{1,0},{2,3},{3,2},{4,5},{5,4},{6,7},{7,6},{8,9},{9,8},{10,11... | collective-permute-start | bytes 30728 | tf_op jit(solution)/shard_map/ppermute | solution.py:11
  63.2 3.8 %collective-permute-start.1 = (bf16[8,1280]{1,0:T(8,128)(2,1)S(1)}, bf16[8,1280]{1,0:T(8,128)(2,1)S(1)}, u32[]{:S(2)}, u32[]{:S(2)}) collective-permute-start(bf16[8,1280]{1,0:T(8,128)(2,1)S(1)} %maximum_select_fusion.5), channel_id=1, source_target_pairs={{0,2},{1,3},{2,0},{3,1},{4,6},{5,7},{6,4},{7,5},{8,10},{9,11},{10,... | collective-permute-start | bytes 61448 | tf_op jit(solution)/shard_map/ppermute | solution.py:11
  67.1 1.3 %collective-permute-start.2 = (bf16[16,1280]{1,0:T(8,128)(2,1)S(1)}, bf16[16,1280]{1,0:T(8,128)(2,1)S(1)}, u32[]{:S(2)}, u32[]{:S(2)}) collective-permute-start(bf16[16,1280]{1,0:T(8,128)(2,1)S(1)} %maximum_select_fusion.4), channel_id=1, source_target_pairs={{0,4},{1,5},{2,6},{3,7},{4,0},{5,1},{6,2},{7,3},{8,12},{9,13},{10,... | collective-permute-start | bytes 122888 | tf_op jit(solution)/shard_map/ppermute | solution.py:11
  68.4 4.6 %collective-permute-start.3 = (bf16[32,1280]{1,0:T(8,128)(2,1)S(1)}, bf16[32,1280]{1,0:T(8,128)(2,1)S(1)}, u32[]{:S(2)}, u32[]{:S(2)}) collective-permute-start(bf16[32,1280]{1,0:T(8,128)(2,1)S(1)} %maximum_select_fusion.3), channel_id=1, source_target_pairs={{0,8},{1,9},{2,10},{3,11},{4,12},{5,13},{6,14},{7,15},{8,0},{9,1},... | collective-permute-start | bytes 245768 | tf_op jit(solution)/shard_map/ppermute | solution.py:11
  73.0 9.9 %collective-permute-start.4 = (bf16[64,1280]{1,0:T(8,128)(2,1)S(1)}, bf16[64,1280]{1,0:T(8,128)(2,1)S(1)}, u32[]{:S(2)}, u32[]{:S(2)}) collective-permute-start(bf16[64,1280]{1,0:T(8,128)(2,1)S(1)} %maximum_select_fusion.2), channel_id=1, source_target_pairs={{0,16},{1,17},{2,18},{3,19},{4,20},{5,21},{6,22},{7,23},{8,24},{9,... | collective-permute-start | bytes 491528 | tf_op jit(solution)/shard_map/ppermute | solution.py:11
